TPU v7x, 32 devices: a whole 2x2x4 slice. The times are simulated.
32 devices in a mesh: dp: 8 (over z, y), fsdp: 4 (over x, core).
Axes of the slice: x: 2, y: 2, z: 4, core: 2. Of those that a mesh axis runs over, the one named last changes fastest.
Arguments:
- keys: bfloat16 [256, 8, 896], P(('dp', 'fsdp')), may hold values from -8 to 8
- residual: bfloat16 [256, 8, 896], P(('dp', 'fsdp')), may hold values from -6 to 6
- se_reduce: bfloat16 [896, 224], P('fsdp'), may hold values from -0.625 to 0.625
- se_expand: bfloat16 [896, 224], P('fsdp'), may hold values from -1.25 to 1.25
- conv_weight: bfloat16 [3, 896, 896], P(None, 'fsdp'), may hold values from -0.1875 to 0.1875
- bn_gain: float32 [896], replicated, may hold values from 0.1 to 1.9
- bn_bias: float32 [896], replicated, may hold values from -3 to 3
- shuffle: int32 [256], P(('dp', 'fsdp')), may hold values from 0 to 63, as said below
- unshuffle: int32 [256], P(('dp', 'fsdp')), may hold values from 0 to 63, as said below
Outputs:
- encoded: bfloat16 [256, 8, 896], P(('dp', 'fsdp'))
Inputs may be any that keep to these rules, and one draw needn't show every extreme that they name: `shuffle`: A permutation of the 64 positions within each group of devices sharing an fsdp index (positions ordered by dp index, then by image); each device sends exactly 1 of its images to every device of its group. `unshuffle`: the inverse of shuffle within each group.
All inputs are finite; a program needn't handle non-finite values.
Results may differ from a plain program's by a relative error of at most 0.013.
Values may be sent and summed in bfloat16 or wider, within the bound.
A program may use at most 64 MiB of HBM per device.

v0:
```python
import jax
import jax.numpy as jnp
from jax import lax
from jax.sharding import PartitionSpec as P

epsilon = 1e-05


def project_rows(flat, weight_rows):
    return jnp.dot(
        flat,
        lax.all_gather(weight_rows, "fsdp", axis=0, tiled=True),
        preferred_element_type=jnp.float32,
    )


def encode_block(batch_block, reduce_full, expand_full, conv_weight):
    images, positions, channels = batch_block.shape
    layers = conv_weight.shape[0]
    flat = batch_block.reshape(images * positions, channels)
    for layer in range(layers - 1):
        flat = jax.nn.relu(project_rows(flat, conv_weight[layer])).astype(jnp.bfloat16)
    entry = flat.reshape(images, positions, channels)
    pooled = jnp.mean(entry, axis=1, dtype=jnp.float32).astype(jnp.bfloat16)
    squeeze_act = jax.nn.relu(
        jnp.dot(pooled, reduce_full, preferred_element_type=jnp.float32)
    ).astype(jnp.bfloat16)
    excite = jax.nn.sigmoid(
        lax.dot_general(
            squeeze_act, expand_full, (((1,), (1,)), ((), ())), preferred_element_type=jnp.float32
        )
    )
    scaled = (entry * excite[:, None, :]).astype(jnp.bfloat16).reshape(images * positions, channels)
    projected = project_rows(scaled, conv_weight[layers - 1])
    return projected.reshape(images, positions, channels)


def local(keys, residual, se_reduce, se_expand, conv_weight, bn_gain, bn_bias, shuffle, unshuffle):
    images, positions, channels = keys.shape
    count = images * positions
    reduce_full, expand_full = (
        lax.all_gather(se_reduce, "fsdp", axis=0, tiled=True),
        lax.all_gather(se_expand, "fsdp", axis=0, tiled=True),
    )
    send_order = jnp.argsort(shuffle)
    back_order = jnp.argsort(send_order)
    outgoing = jnp.take(keys, send_order, axis=0)
    arrived = lax.all_to_all(outgoing, "dp", split_axis=0, concat_axis=0, tiled=True)
    projected = encode_block(arrived, reduce_full, expand_full, conv_weight)
    row_sums = jnp.sum(projected, axis=(0, 1))
    square_sums = jnp.sum(projected * projected, axis=(0, 1))
    mean_rows = row_sums / count
    variance = square_sums / count - mean_rows * mean_rows
    scale_rows = lax.rsqrt(variance + epsilon) * bn_gain
    normed_here = ((projected - mean_rows) * scale_rows + bn_bias).astype(jnp.bfloat16)
    returned = lax.all_to_all(normed_here, "dp", split_axis=0, concat_axis=0, tiled=True)
    normed = jnp.take(returned, back_order, axis=0)
    encoded = jax.nn.relu(normed.astype(jnp.float32) + residual.astype(jnp.float32))
    return encoded.astype(jnp.bfloat16)


def solution(mesh):
    placed = (
        P(("dp", "fsdp"), None, None),
        P(("dp", "fsdp"), None, None),
        P("fsdp", None),
        P("fsdp", None),
        P(None, "fsdp", None),
        P(),
        P(),
        P(("dp", "fsdp")),
        P(("dp", "fsdp")),
    )
    return jax.shard_map(
        local, mesh=mesh, in_specs=placed, out_specs=P(("dp", "fsdp"), None, None), check_vma=False
    )
```

profile of v0, /device:TPU:0, one launch (start us, length us, event | category | flops | bytes accessed | tf_op | source)
XLA Modules:
  0.0 100.1 jit_solution(3672770266905854364)
XLA Ops:
  6.5 0.0 copy-start
  6.5 0.0 all-gather.7.cloned.1.call-start
  6.5 2.4 %fusion.42 = (bf16[1,224,896]{2,1,0:T(8,128)(2,1)}, bf16[1,224,896]{2,1,0:T(8,128)(2,1)}, bf16[1,224,896]{2,1,0:T(8,128)(2,1)}) fusion(bf16[3,224,896]{2,1,0:T(8,128)(2,1)} %param.15), kind=kLoop, calls=%fused_computation.45 | loop fusion | bytes 2408448 | tf_op jit(solution)/shard_map/slice | solution.py:22
  8.9 0.0 all-gather.7.cloned.1.call-update
  9.0 0.0 all-gather.9.cloned.1.call-start
  9.0 0.7 all-gather.9.cloned.1.call-update
  9.7 0.0 all-gather.11.cloned.1.call-start
  9.8 0.7 all-gather.11.cloned.1.call-update
  10.5 0.0 copy-done.6
  10.5 1.0 sort.31
  11.5 0.0 copy-done
  11.5 0.6 gather_fusion
  12.0 0.7 broadcast_select_fusion
  12.8 7.3 %all-to-all-start = ((bf16[8,8,896]{2,1,0:T(8,128)(2,1)}), bf16[8,8,896]{2,1,0:T(8,128)(2,1)S(1)}, u32[]{:S(2)}, u32[]{:S(2)}) async-start(bf16[8,8,896]{2,1,0:T(8,128)(2,1)} %broadcast_select_fusion), calls=%async_computation | async-start | bytes 229376 | tf_op jit(solution)/shard_map/all_to_all | solution.py:48
  20.1 1.0 sort.32
  21.1 0.0 copy-done.1
  21.1 9.7 %all_gather.17 = bf16[896,224]{1,0:T(8,128)(2,1)S(1)} all-gather(bf16[224,224]{1,0:T(8,128)(2,1)S(1)} %copy-done.1), channel_id=1, replica_groups=mesh['dp'=8,'fsdp'=4] {'fsdp'}, dimensions={0}, use_global_device_ids=true | all-gather | bytes 501760 | tf_op jit(solution)/shard_map/all_gather | solution.py:42
  30.8 6.9 %all_gather.18 = bf16[896,224]{1,0:T(8,128)(2,1)S(1)} all-gather(bf16[224,224]{1,0:T(8,128)(2,1)S(1)} %copy-done.2), channel_id=1, replica_groups=mesh['dp'=8,'fsdp'=4] {'fsdp'}, dimensions={0}, use_global_device_ids=true | all-gather | bytes 501760 | tf_op jit(solution)/shard_map/all_gather | solution.py:43
  37.7 0.0 all-to-all-done
  37.7 17.8 %all-gather.9.cloned.1.call-done = bf16[1,896,896]{2,1,0:T(8,128)(2,1)} async-done(((bf16[1,224,896]{2,1,0:T(8,128)(2,1)}), bf16[1,896,896]{2,1,0:T(8,128)(2,1)}) %all-gather.9.cloned.1.call-update) | async-done | bytes 1605648 | tf_op jit(solution)/shard_map/all_gather | solution.py:12
  55.6 2.6 %bitcast_reduce_fusion = (f32[8,896]{1,0:T(8,128)S(1)}, f32[64,896]{1,0:T(8,128)S(1)}) fusion(bf16[1,896,896]{2,1,0:T(8,128)(2,1)} %all-gather.9.cloned.1.call-done, bf16[1,896,896]{2,1,0:T(8,128)(2,1)} %all-gather.7.cloned.1.call-done, bf16[8,8,896]{2,1,0:T(8,128)(2,1)S(1)} %all-to-all-done), kind=kOutput, calls=%fused_computation.21 | convolution fusion | flops 205857792 | bytes 3584000 | tf_op jit(solution)/shard_map/dot_general | solution.py:10
  58.2 0.0 copy-start.5
  58.2 0.0 copy-start.4
  58.2 0.4 fusion.25
  58.6 18.4 %all-gather.11.cloned.1.call-done = bf16[1,896,896]{2,1,0:T(8,128)(2,1)} async-done(((bf16[1,224,896]{2,1,0:T(8,128)(2,1)}), bf16[1,896,896]{2,1,0:T(8,128)(2,1)}) %all-gather.11.cloned.1.call-update) | async-done | bytes 1605648 | tf_op jit(solution)/shard_map/all_gather | solution.py:12
  77.0 1.8 %fusion.41 = (f32[896]{0:T(1024)S(1)}, f32[896]{0:T(1024)S(1)}, f32[8,8,896]{2,1,0:T(8,128)S(1)}) fusion(bf16[1,896,896]{2,1,0:T(8,128)(2,1)} %all-gather.11.cloned.1.call-done, f32[64,896]{1,0:T(8,128)S(1)} %get-tuple-element.18, f32[8,896]{1,0:T(8,128)S(1)} %fusion.25), kind=kOutput, calls=%fused_computation.44 | convolution fusion | flops 103045376 | bytes 2100224 | tf_op jit(solution)/shard_map/dot_general | solution.py:10
  78.8 0.7 add_convert_fusion
  79.5 5.5 %all-to-all-start.1 = ((bf16[8,8,896]{2,1,0:T(8,128)(2,1)}), bf16[8,8,896]{2,1,0:T(8,128)(2,1)S(1)}, u32[]{:S(2)}, u32[]{:S(2)}) async-start(bf16[8,8,896]{2,1,0:T(8,128)(2,1)} %add_convert_fusion), calls=%async_computation.1 | async-start | bytes 229376 | tf_op jit(solution)/shard_map/all_to_all | solution.py:56
  85.0 7.2 %all-to-all-done.1 = bf16[8,8,896]{2,1,0:T(8,128)(2,1)S(1)} async-done(((bf16[8,8,896]{2,1,0:T(8,128)(2,1)}), bf16[8,8,896]{2,1,0:T(8,128)(2,1)S(1)}, u32[]{:S(2)}, u32[]{:S(2)}) %all-to-all-start.1) | async-done | bytes 114720 | tf_op jit(solution)/shard_map/all_to_all | solution.py:56
  92.3 0.6 gather_fusion.1
  92.8 0.0 copy-done.3
  92.8 0.8 maximum_convert_fusion
  (17 shorter events, 0.1 us)
Async XLA Ops:
  6.5 4.9 %copy-start = (bf16[8,8,896]{2,1,0:T(8,128)(2,1)S(1)}, bf16[8,8,896]{2,1,0:T(8,128)(2,1)}, u32[]{:S(2)}) copy-start(bf16[8,8,896]{2,1,0:T(8,128)(2,1)} %param.11) | copy-start | bytes 344068
  6.5 3.9 %copy-start.6 = (s32[8]{0:T(128)S(1)}, s32[8]{0:T(128)}, u32[]{:S(2)}) copy-start(s32[8]{0:T(128)} %param.18) | copy-start | bytes 100
  6.5 14.5 %copy-start.1 = (bf16[224,224]{1,0:T(8,128)(2,1)S(1)}, bf16[224,224]{1,0:T(8,128)(2,1)}, u32[]{:S(2)}) copy-start(bf16[224,224]{1,0:T(8,128)(2,1)} %param.13) | copy-start | bytes 301060
  6.5 31.2 %all-gather.7.cloned.1.call-start = ((), (), s32[]{:S(2)}) async-start(), calls=%async_computation.2 | async-start | bytes 2007040 | tf_op jit(solution)/shard_map/all_gather | solution.py:12
  8.9 21.8 %copy-start.2 = (bf16[224,224]{1,0:T(8,128)(2,1)S(1)}, bf16[224,224]{1,0:T(8,128)(2,1)}, u32[]{:S(2)}) copy-start(bf16[224,224]{1,0:T(8,128)(2,1)} %param.14) | copy-start | bytes 301060
  9.0 46.6 %all-gather.9.cloned.1.call-start = ((), (), s32[]{:S(2)}) async-start(), calls=%async_computation.3 | async-start | bytes 2007040 | tf_op jit(solution)/shard_map/all_gather | solution.py:12
  9.7 67.3 %all-gather.11.cloned.1.call-start = ((), (), s32[]{:S(2)}) async-start(), calls=%async_computation.4 | async-start | bytes 2007040 | tf_op jit(solution)/shard_map/all_gather | solution.py:12
  12.8 24.9 %all-to-all-start = ((bf16[8,8,896]{2,1,0:T(8,128)(2,1)}), bf16[8,8,896]{2,1,0:T(8,128)(2,1)S(1)}, u32[]{:S(2)}, u32[]{:S(2)}) async-start(bf16[8,8,896]{2,1,0:T(8,128)(2,1)} %broadcast_select_fusion), calls=%async_computation | async-start | bytes 229376 | tf_op jit(solution)/shard_map/all_to_all | solution.py:48
  58.2 20.6 %copy-start.5 = (f32[896]{0:T(1024)S(1)}, f32[896]{0:T(1024)}, u32[]{:S(2)}) copy-start(f32[896]{0:T(1024)} %param.16) | copy-start | bytes 10756
  58.2 20.6 %copy-start.4 = (f32[896]{0:T(1024)S(1)}, f32[896]{0:T(1024)}, u32[]{:S(2)}) copy-start(f32[896]{0:T(1024)} %param.17) | copy-start | bytes 10756
  58.6 34.2 %copy-start.3 = (bf16[8,8,896]{2,1,0:T(8,128)(2,1)S(1)}, bf16[8,8,896]{2,1,0:T(8,128)(2,1)}, u32[]{:S(2)}) copy-start(bf16[8,8,896]{2,1,0:T(8,128)(2,1)} %param.12) | copy-start | bytes 344068
  79.5 12.8 %all-to-all-start.1 = ((bf16[8,8,896]{2,1,0:T(8,128)(2,1)}), bf16[8,8,896]{2,1,0:T(8,128)(2,1)S(1)}, u32[]{:S(2)}, u32[]{:S(2)}) async-start(bf16[8,8,896]{2,1,0:T(8,128)(2,1)} %add_convert_fusion), calls=%async_computation.1 | async-start | bytes 229376 | tf_op jit(solution)/shard_map/all_to_all | solution.py:56
Sparse Core Ops, SparseCore 0:
  9.1 24.9 all-gather.6
  35.7 19.8 all-gather.8
  57.1 19.8 all-gather.10
where the time goes:
time: 100 us
  waiting for transfers between devices  44.8 us (45%)
  blocking collectives  16.6 us (17%)
  between operations  13.2 us (13%)
  starting transfers between devices  12.9 us (13%)
  matrix products  4.83 us (5%)
  other arithmetic  4.17 us (4%)
  local copies, waits for them, and re-layouts  3.57 us (4%)
    all_gather x3, waiting for transfers between devices, project_rows(): lax.all_gather(weight_rows, 'fsdp', axis=0, tiled=True)  36.2 us
    all_gather x1, blocking collectives, local(): lax.all_gather(se_reduce, 'fsdp', axis=0, tiled=True)  9.71 us
    all_to_all x1, starting transfers between devices, local(): lax.all_to_all(outgoing, 'dp', split_axis=0, concat_axis=0, tiled=True)  7.28 us
    all_to_all x1, waiting for transfers between devices, local(): lax.all_to_all(normed_here, 'dp', split_axis=0, concat_axis=0, tiled=True)  7.23 us
    all_gather x1, blocking collectives, local(): lax.all_gather(se_expand, 'fsdp', axis=0, tiled=True)  6.94 us
    all_to_all x1, starting transfers between devices, local(): lax.all_to_all(normed_here, 'dp', split_axis=0, concat_axis=0, tiled=True)  5.52 us
    dot_general x2, matrix products, project_rows(): jnp.dot(flat, lax.all_gather(weight_rows, 'fsdp', axis=0, tiled=True), pr...  4.4 us
    slice x1, local copies, waits for them, and re-layouts, encode_block(): conv_weight[layer]  2.4 us
  transfers between devices with their start and end apart: 5, of which 3 were waited for; matrix products, arithmetic and copies ran while one was open for 6% of the time, Pallas kernels for 0%

commit v1 on v0

--- a/solution.py
+++ b/solution.py
@@ -6,12 +6,20 @@
 epsilon = 1e-05
 
 
+def ring_gather(value, axis, dim):
+    ways, here, step = (lax.axis_size(axis), lax.axis_index(axis), value.shape[dim])
+    dims = [n * ways if d == dim else n for d, n in enumerate(value.shape)]
+    full = lax.dynamic_update_slice_in_dim(
+        jnp.zeros(dims, value.dtype), value, here * step, axis=dim
+    )
+    for far in range(1, ways):
+        value = lax.ppermute(value, axis, [(d, (d + 1) % ways) for d in range(ways)])
+        full = lax.dynamic_update_slice_in_dim(full, value, (here - far) % ways * step, axis=dim)
+    return full
+
+
 def project_rows(flat, weight_rows):
-    return jnp.dot(
-        flat,
-        lax.all_gather(weight_rows, "fsdp", axis=0, tiled=True),
-        preferred_element_type=jnp.float32,
-    )
+    return jnp.dot(flat, ring_gather(weight_rows, "fsdp", 0), preferred_element_type=jnp.float32)
 
 
 def encode_block(batch_block, reduce_full, expand_full, conv_weight):

time: 100 us -> 80.4 us (0.80)
  waiting for transfers between devices: 44.8 us -> 18.3 us
  local copies, waits for them, and re-layouts: 3.57 us -> 17.2 us
  between operations: 13.2 us -> 0.21 us
  starting transfers between devices: 12.9 us -> 16.2 us
  blocking collectives: 16.6 us -> 18.2 us
    all_gather x3 -> x0, waiting for transfers between devices: 36.2 us -> none  [project_rows(): lax.all_gather(weight_rows, 'fsdp', axis=0, tiled=True)]
    dynamic_update_slice x0 -> x12, local copies, waits for them, and re-layouts: none -> 11.5 us  [the longest x9 9.65 us: ring_gather(): lax.dynamic_update_slice_in_dim(full, value, (here - far) % ways * step,...]
    ppermute x0 -> x9, waiting for transfers between devices: none -> 11.1 us  [ring_gather(): lax.ppermute(value, axis, [(d, (d + 1) % ways) for d in range(ways)])]
    ppermute x0 -> x9, starting transfers between devices: none -> 4.33 us  [ring_gather(): lax.ppermute(value, axis, [(d, (d + 1) % ways) for d in range(ways)])]
    all_gather x1, blocking collectives: 6.94 us -> 10.6 us  [local(): lax.all_gather(se_expand, 'fsdp', axis=0, tiled=True)]
    slice x1 -> x0, local copies, waits for them, and re-layouts: 2.4 us -> none  [encode_block(): conv_weight[layer]]
    squeeze x0 -> x1, local copies, waits for them, and re-layouts: none -> 2.32 us  [encode_block(): conv_weight[layer]]
    all_gather x1, blocking collectives: 9.71 us -> 7.64 us  [local(): lax.all_gather(se_reduce, 'fsdp', axis=0, tiled=True)]
  transfers between devices with their start and end apart: 5 -> 11, of which waited for: 3 -> 5; matrix products, arithmetic and copies ran while one was open for 6% -> 25% of each run, Pallas kernels for 0% -> 0%
where the time goes in v1:
time: 80.4 us; the launch traced here: 79.7 us
  waiting for transfers between devices  18.3 us (23%)
  blocking collectives  18.2 us (23%)
  local copies, waits for them, and re-layouts  17.2 us (21%)
  starting transfers between devices  16.2 us (20%)
  matrix products  4.78 us (6%)
  other arithmetic  4.76 us (6%)
    ppermute x9, waiting for transfers between devices, ring_gather(): lax.ppermute(value, axis, [(d, (d + 1) % ways) for d in range(ways)])  11.1 us
    all_gather x1, blocking collectives, local(): lax.all_gather(se_expand, 'fsdp', axis=0, tiled=True)  10.6 us
    dynamic_update_slice x9, local copies, waits for them, and re-layouts, ring_gather(): lax.dynamic_update_slice_in_dim(full, value, (here - far) % ways * step,...  9.65 us
    all_gather x1, blocking collectives, local(): lax.all_gather(se_reduce, 'fsdp', axis=0, tiled=True)  7.64 us
    all_to_all x1, waiting for transfers between devices, local(): lax.all_to_all(normed_here, 'dp', split_axis=0, concat_axis=0, tiled=True)  7.21 us
    all_to_all x1, starting transfers between devices, local(): lax.all_to_all(normed_here, 'dp', split_axis=0, concat_axis=0, tiled=True)  6 us
    all_to_all x1, starting transfers between devices, local(): lax.all_to_all(outgoing, 'dp', split_axis=0, concat_axis=0, tiled=True)  5.83 us
    ppermute x9, starting transfers between devices, ring_gather(): lax.ppermute(value, axis, [(d, (d + 1) % ways) for d in range(ways)])  4.33 us
  transfers between devices with their start and end apart: 11, of which 5 were waited for; matrix products, arithmetic and copies ran while one was open for 25% of the time, Pallas kernels for 0%

profile of v1, /device:TPU:0, one launch (start us, length us, event | category | flops | bytes accessed | tf_op | source)
XLA Modules:
  0.0 79.7 jit_solution(5614869759038604212)
XLA Ops:
  0.0 2.3 %slice_bitcast_fusion.2 = (bf16[224,896]{1,0:T(8,128)(2,1)}, bf16[224,896]{1,0:T(8,128)(2,1)}, bf16[224,896]{1,0:T(8,128)(2,1)}) fusion(bf16[3,224,896]{2,1,0:T(8,128)(2,1)} %param.15), kind=kLoop, calls=%fused_computation.17 | loop fusion | bytes 2408448 | tf_op jit(solution)/shard_map/squeeze | solution.py:30
  2.8 2.6 %collective-permute-start = (bf16[224,896]{1,0:T(8,128)(2,1)}, bf16[224,896]{1,0:T(8,128)(2,1)}, u32[]{:S(2)}, u32[]{:S(2)}) collective-permute-start(bf16[224,896]{1,0:T(8,128)(2,1)} %get-tuple-element.12), channel_id=1, source_target_pairs={{0,1},{1,2},{2,3},{3,0},{4,5},{5,6},{6,7},{7,4},{8,9},{9,10},{10,1... | collective-permute-start | bytes 1204232 | tf_op jit(solution)/shard_map/ppermute | solution.py:16
  5.4 1.0 %sort.31 = (s32[8]{0:T(128)}, s32[8]{0:T(128)S(1)}) sort(s32[8]{0:T(128)S(1)} %copy-done.7, s32[8]{0:T(128)S(1)} %iota.7), dimensions={0}, to_apply=%region_0.0 | sort | flops 24 | bytes 128 | tf_op jit(solution)/shard_map/jit(argsort)/sort | solution.py:53
  6.4 0.6 gather_fusion
  7.0 0.7 broadcast_select_fusion
  7.7 5.8 %all-to-all-start = ((bf16[8,8,896]{2,1,0:T(8,128)(2,1)}), bf16[8,8,896]{2,1,0:T(8,128)(2,1)}, u32[]{:S(2)}, u32[]{:S(2)}) async-start(bf16[8,8,896]{2,1,0:T(8,128)(2,1)} %broadcast_select_fusion), calls=%async_computation | async-start | bytes 229376 | tf_op jit(solution)/shard_map/all_to_all | solution.py:56
  13.8 1.3 %broadcast.36.clone.2 = bf16[896,896]{1,0:T(8,128)(2,1)} broadcast(bf16[]{:T(256)} %constant.68.clone.1), dimensions={} | broadcast | bytes 1605634 | tf_op jit(solution)/shard_map/broadcast.13
  15.0 0.8 constant_dynamic-update-slice_fusion.11
  15.8 1.0 %sort.32 = (s32[8]{0:T(128)}, s32[8]{0:T(128)S(1)}) sort(s32[8]{0:T(128)S(1)} %get-tuple-element.8, s32[8]{0:T(128)S(1)} %iota.8), dimensions={0}, to_apply=%region_4.6 | sort | flops 24 | bytes 128 | tf_op jit(solution)/shard_map/jit(argsort)/sort | solution.py:54
  17.4 7.6 %all_gather.6 = bf16[896,224]{1,0:T(8,128)(2,1)} all-gather(bf16[224,224]{1,0:T(8,128)(2,1)S(1)} %copy-done.2), channel_id=1, replica_groups=mesh['dp'=8,'fsdp'=4] {'fsdp'}, dimensions={0}, use_global_device_ids=true | all-gather | bytes 501760 | tf_op jit(solution)/shard_map/all_gather | solution.py:50
  25.1 1.0 %constant_dynamic-update-slice_fusion.3 = bf16[896,896]{1,0:T(8,128)(2,1)S(1)} fusion(bf16[896,896]{1,0:T(8,128)(2,1)S(1)} %broadcast.36.clone, s32[]{:T(128)S(6)} %select_n.54, bf16[3,224,896]{2,1,0:T(8,128)(2,1)} %param.15), kind=kLoop, calls=%fused_computation.38 | loop fusion | bytes 802820 | tf_op jit(solution)/shard_map/dynamic_update_slice | solution.py:12
  26.6 10.6 %all_gather.7 = bf16[896,224]{1,0:T(8,128)(2,1)} all-gather(bf16[224,224]{1,0:T(8,128)(2,1)S(1)} %copy-done.3), channel_id=1, replica_groups=mesh['dp'=8,'fsdp'=4] {'fsdp'}, dimensions={0}, use_global_device_ids=true | all-gather | bytes 501760 | tf_op jit(solution)/shard_map/all_gather | solution.py:51
  37.3 0.6 collective-permute-start.7
  37.9 0.6 pad_clamp_fusion
  38.5 1.0 %constant_dynamic-update-slice_fusion.6 = bf16[896,896]{1,0:T(8,128)(2,1)S(1)} fusion(bf16[896,896]{1,0:T(8,128)(2,1)S(1)} %constant_dynamic-update-slice_fusion.7, bf16[224,896]{1,0:T(8,128)(2,1)} %collective-permute-done.3, s32[]{:T(128)S(6)} %select_n.56), kind=kLoop, calls=%fused_computation.41 | loop fusion | bytes 802820 | tf_op jit(solution)/shard_map/dynamic_update_slice | solution.py:17
  39.5 1.8 %constant_dynamic-update-slice_fusion.10 = bf16[896,896]{1,0:T(8,128)(2,1)} fusion(bf16[896,896]{1,0:T(8,128)(2,1)} %constant_dynamic-update-slice_fusion.11, bf16[224,896]{1,0:T(8,128)(2,1)} %collective-permute-done, s32[]{:T(128)S(6)} %select_n.56), kind=kLoop, calls=%fused_computation.45 | loop fusion | bytes 802820 | tf_op jit(solution)/shard_map/dynamic_update_slice | solution.py:17
  41.5 1.0 %constant_dynamic-update-slice_fusion.2 = bf16[896,896]{1,0:T(8,128)(2,1)S(1)} fusion(bf16[896,896]{1,0:T(8,128)(2,1)S(1)} %constant_dynamic-update-slice_fusion.3, bf16[224,896]{1,0:T(8,128)(2,1)} %collective-permute-done.6, s32[]{:T(128)S(6)} %select_n.56), kind=kLoop, calls=%fused_computation.37 | loop fusion | bytes 802820 | tf_op jit(solution)/shard_map/dynamic_update_slice | solution.py:17
  42.5 2.2 %collective-permute-done.1 = bf16[224,896]{1,0:T(8,128)(2,1)} collective-permute-done((bf16[224,896]{1,0:T(8,128)(2,1)}, bf16[224,896]{1,0:T(8,128)(2,1)}, u32[]{:S(2)}, u32[]{:S(2)}) %collective-permute-start.1) | collective-permute-done | bytes 401440 | tf_op jit(solution)/shard_map/ppermute | solution.py:16
  44.8 4.3 %collective-permute-done.7 = bf16[224,896]{1,0:T(8,128)(2,1)} collective-permute-done((bf16[224,896]{1,0:T(8,128)(2,1)}, bf16[224,896]{1,0:T(8,128)(2,1)}, u32[]{:S(2)}, u32[]{:S(2)}) %collective-permute-start.7) | collective-permute-done | bytes 401440 | tf_op jit(solution)/shard_map/ppermute | solution.py:16
  49.1 1.0 %constant_dynamic-update-slice_fusion.5 = bf16[896,896]{1,0:T(8,128)(2,1)S(1)} fusion(bf16[896,896]{1,0:T(8,128)(2,1)S(1)} %constant_dynamic-update-slice_fusion.6, bf16[224,896]{1,0:T(8,128)(2,1)} %collective-permute-done.4, s32[]{:T(128)S(6)} %select_n.58), kind=kLoop, calls=%fused_computation.40 | loop fusion | bytes 802820 | tf_op jit(solution)/shard_map/dynamic_update_slice | solution.py:17
  50.1 1.8 %constant_dynamic-update-slice_fusion.9 = bf16[896,896]{1,0:T(8,128)(2,1)} fusion(bf16[896,896]{1,0:T(8,128)(2,1)} %constant_dynamic-update-slice_fusion.10, bf16[224,896]{1,0:T(8,128)(2,1)} %collective-permute-done.1, s32[]{:T(128)S(6)} %select_n.58), kind=kLoop, calls=%fused_computation.44 | loop fusion | bytes 802820 | tf_op jit(solution)/shard_map/dynamic_update_slice | solution.py:17
  51.9 1.0 %constant_dynamic-update-slice_fusion.1 = bf16[896,896]{1,0:T(8,128)(2,1)S(1)} fusion(bf16[896,896]{1,0:T(8,128)(2,1)S(1)} %constant_dynamic-update-slice_fusion.2, bf16[224,896]{1,0:T(8,128)(2,1)} %collective-permute-done.7, s32[]{:T(128)S(6)} %select_n.58), kind=kLoop, calls=%fused_computation.36 | loop fusion | bytes 802820 | tf_op jit(solution)/shard_map/dynamic_update_slice | solution.py:17
  53.3 4.3 %collective-permute-done.2 = bf16[224,896]{1,0:T(8,128)(2,1)S(1)} collective-permute-done((bf16[224,896]{1,0:T(8,128)(2,1)}, bf16[224,896]{1,0:T(8,128)(2,1)S(1)}, u32[]{:S(2)}, u32[]{:S(2)}) %collective-permute-start.2) | collective-permute-done | bytes 401440 | tf_op jit(solution)/shard_map/ppermute | solution.py:16
  57.6 0.8 constant_dynamic-update-slice_fusion.8
  58.4 2.8 %bitcast_reduce_fusion = (f32[8,896]{1,0:T(8,128)}, f32[64,896]{1,0:T(8,128)S(1)}) fusion(bf16[896,896]{1,0:T(8,128)(2,1)S(1)} %constant_dynamic-update-slice_fusion.4, bf16[896,896]{1,0:T(8,128)(2,1)} %constant_dynamic-update-slice_fusion.8, bf16[8,8,896]{2,1,0:T(8,128)(2,1)} %all-to-all-done), kind=kOutput, calls=%fused_computation.20 | convolution fusion | flops 205857792 | bytes 3584000 | tf_op jit(solution)/shard_map/dot_general | solution.py:22
  61.2 1.6 %fusion.7 = f32[8,896]{1,0:T(8,128)S(1)} fusion(bf16[896,224]{1,0:T(8,128)(2,1)} %all_gather.7, bf16[896,224]{1,0:T(8,128)(2,1)} %all_gather.6, f32[8,896]{1,0:T(8,128)} %get-tuple-element.17), kind=kOutput, calls=%fused_computation.12 | convolution fusion | flops 6461952 | bytes 860160 | tf_op jit(solution)/shard_map/dot_general | solution.py:37
  62.8 1.1 %constant_dynamic-update-slice_fusion = bf16[896,896]{1,0:T(8,128)(2,1)S(1)} fusion(bf16[896,896]{1,0:T(8,128)(2,1)S(1)} %constant_dynamic-update-slice_fusion.1, bf16[224,896]{1,0:T(8,128)(2,1)} %collective-permute-done.8, s32[]{:T(128)S(6)} %select_n.60), kind=kLoop, calls=%fused_computation.35 | loop fusion | bytes 802820 | tf_op jit(solution)/shard_map/dynamic_update_slice | solution.py:17
  64.3 0.7 add_convert_fusion
  65.0 6.0 %all-to-all-start.1 = ((bf16[8,8,896]{2,1,0:T(8,128)(2,1)}), bf16[8,8,896]{2,1,0:T(8,128)(2,1)S(1)}, u32[]{:S(2)}, u32[]{:S(2)}) async-start(bf16[8,8,896]{2,1,0:T(8,128)(2,1)} %add_convert_fusion), calls=%async_computation.1 | async-start | bytes 229376 | tf_op jit(solution)/shard_map/all_to_all | solution.py:64
  71.0 7.2 %all-to-all-done.1 = bf16[8,8,896]{2,1,0:T(8,128)(2,1)S(1)} async-done(((bf16[8,8,896]{2,1,0:T(8,128)(2,1)}), bf16[8,8,896]{2,1,0:T(8,128)(2,1)S(1)}, u32[]{:S(2)}, u32[]{:S(2)}) %all-to-all-start.1) | async-done | bytes 114720 | tf_op jit(solution)/shard_map/all_to_all | solution.py:64
  78.2 0.7 gather_fusion.1
  78.9 0.8 maximum_convert_fusion
  (47 shorter events, 2.8 us)
Async XLA Ops:
  0.0 6.4 %copy-start = (bf16[8,8,896]{2,1,0:T(8,128)(2,1)S(1)}, bf16[8,8,896]{2,1,0:T(8,128)(2,1)}, u32[]{:S(2)}) copy-start(bf16[8,8,896]{2,1,0:T(8,128)(2,1)} %param.11) | copy-start | bytes 344068
  0.0 5.4 %copy-start.7 = (s32[8]{0:T(128)S(1)}, s32[8]{0:T(128)}, u32[]{:S(2)}) copy-start(s32[8]{0:T(128)} %param.18) | copy-start | bytes 100
  2.3 11.3 %copy-start.1 = (bf16[3,224,896]{2,1,0:T(8,128)(2,1)S(1)}, bf16[3,224,896]{2,1,0:T(8,128)(2,1)}, u32[]{:S(2)}) copy-start(bf16[3,224,896]{2,1,0:T(8,128)(2,1)} %param.15) | copy-start | bytes 3612676
  2.3 23.9 %collective-permute-start.3 = (bf16[224,896]{1,0:T(8,128)(2,1)}, bf16[224,896]{1,0:T(8,128)(2,1)}, u32[]{:S(2)}, u32[]{:S(2)}) collective-permute-start(bf16[224,896]{1,0:T(8,128)(2,1)} %get-tuple-element.14), channel_id=1, source_target_pairs={{0,1},{1,2},{2,3},{3,0},{4,5},{5,6},{6,7},{7,4},{8,9},{9,10},{10,1... | collective-permute-start | bytes 1204232 | tf_op jit(solution)/shard_map/ppermute | solution.py:16
  2.8 34.4 %collective-permute-start = (bf16[224,896]{1,0:T(8,128)(2,1)}, bf16[224,896]{1,0:T(8,128)(2,1)}, u32[]{:S(2)}, u32[]{:S(2)}) collective-permute-start(bf16[224,896]{1,0:T(8,128)(2,1)} %get-tuple-element.12), channel_id=1, source_target_pairs={{0,1},{1,2},{2,3},{3,0},{4,5},{5,6},{6,7},{7,4},{8,9},{9,10},{10,1... | collective-permute-start | bytes 1204232 | tf_op jit(solution)/shard_map/ppermute | solution.py:16
  7.7 50.7 %all-to-all-start = ((bf16[8,8,896]{2,1,0:T(8,128)(2,1)}), bf16[8,8,896]{2,1,0:T(8,128)(2,1)}, u32[]{:S(2)}, u32[]{:S(2)}) async-start(bf16[8,8,896]{2,1,0:T(8,128)(2,1)} %broadcast_select_fusion), calls=%async_computation | async-start | bytes 229376 | tf_op jit(solution)/shard_map/all_to_all | solution.py:56
  13.5 23.8 %collective-permute-start.6 = (bf16[224,896]{1,0:T(8,128)(2,1)}, bf16[224,896]{1,0:T(8,128)(2,1)}, u32[]{:S(2)}, u32[]{:S(2)}) collective-permute-start(bf16[224,896]{1,0:T(8,128)(2,1)} %get-tuple-element.13), channel_id=1, source_target_pairs={{0,1},{1,2},{2,3},{3,0},{4,5},{5,6},{6,7},{7,4},{8,9},{9,10},{10,1... | collective-permute-start | bytes 1204232 | tf_op jit(solution)/shard_map/ppermute | solution.py:16
  13.7 3.7 %copy-start.2 = (bf16[224,224]{1,0:T(8,128)(2,1)S(1)}, bf16[224,224]{1,0:T(8,128)(2,1)}, u32[]{:S(2)}) copy-start(bf16[224,224]{1,0:T(8,128)(2,1)} %param.13) | copy-start | bytes 301060
  15.8 10.8 %copy-start.3 = (bf16[224,224]{1,0:T(8,128)(2,1)S(1)}, bf16[224,224]{1,0:T(8,128)(2,1)}, u32[]{:S(2)}) copy-start(bf16[224,224]{1,0:T(8,128)(2,1)} %param.14) | copy-start | bytes 301060
  16.8 0.5 copy-start.8
  26.2 15.1 %collective-permute-start.4 = (bf16[224,896]{1,0:T(8,128)(2,1)}, bf16[224,896]{1,0:T(8,128)(2,1)}, u32[]{:S(2)}, u32[]{:S(2)}) collective-permute-start(bf16[224,896]{1,0:T(8,128)(2,1)} %collective-permute-done.3), channel_id=1, source_target_pairs={{0,1},{1,2},{2,3},{3,0},{4,5},{5,6},{6,7},{7,4},{8,9},{9,10},{10,1... | collective-permute-start | bytes 1204232 | tf_op jit(solution)/shard_map/ppermute | solution.py:16
  37.2 7.6 %collective-permute-start.1 = (bf16[224,896]{1,0:T(8,128)(2,1)}, bf16[224,896]{1,0:T(8,128)(2,1)}, u32[]{:S(2)}, u32[]{:S(2)}) collective-permute-start(bf16[224,896]{1,0:T(8,128)(2,1)} %collective-permute-done), channel_id=1, source_target_pairs={{0,1},{1,2},{2,3},{3,0},{4,5},{5,6},{6,7},{7,4},{8,9},{9,10},{10,1... | collective-permute-start | bytes 1204232 | tf_op jit(solution)/shard_map/ppermute | solution.py:16
  37.3 11.7 %collective-permute-start.7 = (bf16[224,896]{1,0:T(8,128)(2,1)}, bf16[224,896]{1,0:T(8,128)(2,1)}, u32[]{:S(2)}, u32[]{:S(2)}) collective-permute-start(bf16[224,896]{1,0:T(8,128)(2,1)} %collective-permute-done.6), channel_id=1, source_target_pairs={{0,1},{1,2},{2,3},{3,0},{4,5},{5,6},{6,7},{7,4},{8,9},{9,10},{10,1... | collective-permute-start | bytes 1204232 | tf_op jit(solution)/shard_map/ppermute | solution.py:16
  41.3 11.9 %collective-permute-start.5 = (bf16[224,896]{1,0:T(8,128)(2,1)}, bf16[224,896]{1,0:T(8,128)(2,1)S(1)}, u32[]{:S(2)}, u32[]{:S(2)}) collective-permute-start(bf16[224,896]{1,0:T(8,128)(2,1)} %collective-permute-done.4), channel_id=1, source_target_pairs={{0,1},{1,2},{2,3},{3,0},{4,5},{5,6},{6,7},{7,4},{8,9},{9,10},{10,1... | collective-permute-start | bytes 1204232 | tf_op jit(solution)/shard_map/ppermute | solution.py:16
  44.8 12.8 %collective-permute-start.2 = (bf16[224,896]{1,0:T(8,128)(2,1)}, bf16[224,896]{1,0:T(8,128)(2,1)S(1)}, u32[]{:S(2)}, u32[]{:S(2)}) collective-permute-start(bf16[224,896]{1,0:T(8,128)(2,1)} %collective-permute-done.1), channel_id=1, source_target_pairs={{0,1},{1,2},{2,3},{3,0},{4,5},{5,6},{6,7},{7,4},{8,9},{9,10},{10,1... | collective-permute-start | bytes 1204232 | tf_op jit(solution)/shard_map/ppermute | solution.py:16
  49.1 13.7 %collective-permute-start.8 = (bf16[224,896]{1,0:T(8,128)(2,1)}, bf16[224,896]{1,0:T(8,128)(2,1)}, u32[]{:S(2)}, u32[]{:S(2)}) collective-permute-start(bf16[224,896]{1,0:T(8,128)(2,1)} %collective-permute-done.7), channel_id=1, source_target_pairs={{0,1},{1,2},{2,3},{3,0},{4,5},{5,6},{6,7},{7,4},{8,9},{9,10},{10,1... | collective-permute-start | bytes 1204232 | tf_op jit(solution)/shard_map/ppermute | solution.py:16
  62.8 1.5 %copy-start.6 = (f32[896]{0:T(1024)S(1)}, f32[896]{0:T(1024)}, u32[]{:S(2)}) copy-start(f32[896]{0:T(1024)} %param.16) | copy-start | bytes 10756
  62.8 1.5 %copy-start.5 = (f32[896]{0:T(1024)S(1)}, f32[896]{0:T(1024)}, u32[]{:S(2)}) copy-start(f32[896]{0:T(1024)} %param.17) | copy-start | bytes 10756
  62.8 8.2 %copy-start.9 = (s32[8]{0:T(128)S(1)}, s32[8]{0:T(128)}, u32[]{:S(2)}) copy-start(s32[8]{0:T(128)} %copy-done.8) | copy-start | bytes 100
  63.9 15.0 %copy-start.4 = (bf16[8,8,896]{2,1,0:T(8,128)(2,1)S(1)}, bf16[8,8,896]{2,1,0:T(8,128)(2,1)}, u32[]{:S(2)}) copy-start(bf16[8,8,896]{2,1,0:T(8,128)(2,1)} %param.12) | copy-start | bytes 344068
  65.0 13.2 %all-to-all-start.1 = ((bf16[8,8,896]{2,1,0:T(8,128)(2,1)}), bf16[8,8,896]{2,1,0:T(8,128)(2,1)S(1)}, u32[]{:S(2)}, u32[]{:S(2)}) async-start(bf16[8,8,896]{2,1,0:T(8,128)(2,1)} %add_convert_fusion), calls=%async_computation.1 | async-start | bytes 229376 | tf_op jit(solution)/shard_map/all_to_all | solution.py:64
